TPU v7x, 128 devices: a whole 4x4x4 slice. The times are simulated.
128 devices in a mesh: space: 32 (over z, y, core), mode: 4 (over x).
Axes of the slice: x: 4, y: 4, z: 4, core: 2. Of those that a mesh axis runs over, the one named last changes fastest.
Arguments:
- velocity: float32 [3, 512, 512, 256], P(None, 'space', 'mode'), may hold values from -6 to 6
- basis: float32 [32, 3145728], P('mode', 'space'), may hold values from -42 to 42
- levels: float32 [8], replicated, may hold values from 0.02 to 0.15
- profile_index: int32 [256], replicated, may hold values from 0 to 7
- advect: float32 [256], replicated, may hold values from 0 to 0.4
Outputs:
- modes: float32 [32, 3145728], P('mode', 'space')
- sigma: float32 [32], replicated
Inputs may be any that keep to these rules, and one draw needn't show every extreme that they name: `profile_index`: each entry picks one of the 8 viscosity levels.
All inputs are finite; a program needn't handle non-finite values.
Results may differ from a plain program's by a relative error of at most 0.0055.
Values sent between devices are 32-bit elements; how exact they have to be, the bound alone decides.
No kernel may reach another device: no remote copies, remote signals or barrier semaphores. Data moves between devices by JAX's collectives and lax.ppermute only.
A program may use at most 128 MiB of HBM per device.

v0:
```python
import math
import jax
import jax.numpy as jnp
import numpy as np
from jax import lax
from jax.sharding import PartitionSpec as P

STRIDE = 4
MODES = 32
SWEEPS = 2


def extended(x, sides, width):
    for axis, dim in sides:
        size, length = (lax.axis_size(axis), x.shape[dim])
        up = [(i, (i + 1) % size) for i in range(size)]
        down = [(j, i) for i, j in up]
        last = lax.slice_in_dim(x, length - width, length, axis=dim)
        leading = lax.slice_in_dim(x, 0, width, axis=dim)
        before = lax.ppermute(last, axis, up)
        after = lax.ppermute(leading, axis, down)
        x = jnp.concatenate([before, x, after], axis=dim)
    return x


def profile(levels, profile_index):
    table = (
        profile_index[:, None] == jnp.arange(levels.shape[0], dtype=jnp.int32)[None, :]
    ).astype(jnp.float32)
    viscosity = jnp.sum(table * levels[None, :], axis=1)
    middle = 0.5 * (viscosity[:-1] + viscosity[1:])
    face_up = jnp.concatenate([middle, viscosity[-1:]])
    face_down = jnp.concatenate([viscosity[:1], middle])
    return (viscosity, face_down, face_up)


def advance(field, viscosity, face_down, face_up, advect):
    center = field[:, 1:-1, 1:-1, :]
    east = field[:, 2:, 1:-1, :]
    west = field[:, :-2, 1:-1, :]
    north = field[:, 1:-1, 2:, :]
    south = field[:, 1:-1, :-2, :]
    walled = jnp.pad(center, ((0, 0), (0, 0), (0, 0), (1, 1)))
    upward = walled[..., 2:]
    downward = walled[..., :-2]
    lateral = east + west + north + south - 4.0 * center
    vertical = face_up * (upward - center) - face_down * (center - downward)
    return center + viscosity * lateral + vertical - 0.5 * advect * (east - west)


def coarsen(field):
    components, x_cells, z_cells, y_cells = field.shape
    plane = z_cells * y_cells
    slabs = field.reshape(components * (x_cells // STRIDE), STRIDE * plane)
    along_x = slabs[:, 0:plane]
    for offset in range(1, STRIDE):
        along_x = along_x + slabs[:, offset * plane : (offset + 1) * plane]
    lines = along_x.reshape(
        components * (x_cells // STRIDE) * (z_cells // STRIDE), STRIDE * y_cells
    )
    along_z = lines[:, 0:y_cells]
    for offset in range(1, STRIDE):
        along_z = along_z + lines[:, offset * y_cells : (offset + 1) * y_cells]
    cell_ids = jnp.arange(y_cells, dtype=jnp.int32)[:, None] // STRIDE
    box_ids = jnp.arange(y_cells // STRIDE, dtype=jnp.int32)[None, :]
    summing = (cell_ids == box_ids).astype(jnp.float32)
    boxed = jnp.dot(
        along_z, summing, precision=lax.Precision.HIGHEST, preferred_element_type=jnp.float32
    )
    return (boxed / math.sqrt(STRIDE**3)).reshape(-1)


def with_faces(field):
    return extended(field, (("space", 1), ("mode", 2)), 1)


def round_order(count, turn):
    players = [0] + [1 + (i_pos - 1 + turn) % (count - 1) for i_pos in range(1, count)]
    leading = players[: count // 2]
    trailing = [players[count - 1 - k_pos] for k_pos in range(count // 2)]
    return np.array(leading + trailing)


def reorder_table(count, turn):
    current = round_order(count, turn)
    following = round_order(count, (turn + 1) % (count - 1))
    where_now = np.zeros(count, dtype=np.int64)
    where_now[current] = np.arange(count)
    table = np.zeros((count, count), dtype=np.float32)
    table[where_now[following], np.arange(count)] = 1.0
    return table


def jacobi_sweep(joined, tables):
    count = joined.shape[1]
    half = count // 2
    for turn in range(count - 1):
        col_lead = joined[:, :half]
        col_trail = joined[:, half:]
        rot_lead = col_lead[:count]
        rot_trail = col_trail[:count]
        norm_lead = jnp.sum(rot_lead * rot_lead, axis=0)
        norm_trail = jnp.sum(rot_trail * rot_trail, axis=0)
        inner = jnp.sum(rot_lead * rot_trail, axis=0)
        contrast = norm_trail - norm_lead
        orient = jnp.where(contrast >= 0.0, 1.0, -1.0)
        denominator = jnp.abs(contrast) + jnp.sqrt(contrast * contrast + 4.0 * inner * inner)
        positive = denominator > 0.0
        tangent = jnp.where(
            positive, 2.0 * inner * orient / jnp.where(positive, denominator, 1.0), 0.0
        )
        cosine = 1.0 / jnp.sqrt(1.0 + tangent * tangent)
        sine_part = cosine * tangent
        rotated_pairs = jnp.concatenate(
            [cosine * col_lead - sine_part * col_trail, sine_part * col_lead + cosine * col_trail],
            axis=1,
        )
        joined = jnp.dot(
            rotated_pairs,
            tables[turn],
            precision=lax.Precision.HIGHEST,
            preferred_element_type=jnp.float32,
        )
    return joined


def jacobi(upper):
    count = upper.shape[1]
    start_order = round_order(count, 0)
    back_order = np.zeros(count, dtype=np.int64)
    back_order[start_order] = np.arange(count)
    tables = [jnp.asarray(reorder_table(count, turn)) for turn in range(count - 1)]
    joined = jnp.concatenate([upper, jnp.eye(count, dtype=jnp.float32)], axis=0)[:, start_order]
    joined = lax.fori_loop(
        0, SWEEPS, lambda sweep_index, state: jacobi_sweep(state, tables), joined
    )
    joined = joined[:, back_order]
    return (joined[:count], joined[count:])


def row_products(matrix):
    return lax.dot_general(
        matrix,
        matrix,
        (((1,), (1,)), ((), ())),
        precision=lax.Precision.HIGHEST,
        preferred_element_type=jnp.float32,
    )


def per_device(velocity, basis, levels, profile_index, advect):
    viscosity, face_down, face_up = profile(levels, profile_index)
    first = advance(with_faces(velocity), viscosity, face_down, face_up, advect)
    second = advance(with_faces(first), viscosity, face_down, face_up, advect)
    snapshots = jnp.stack([coarsen(first), coarsen(second)])
    own_rows = jnp.concatenate(
        [snapshots, lax.all_to_all(basis, "mode", split_axis=1, concat_axis=0, tiled=True)], axis=0
    )
    gram = row_products(own_rows)
    lower = jnp.linalg.cholesky(lax.psum(gram, ("space", "mode")))
    rotated, right_vecs = jacobi(lower.T)
    kept = rotated[:, :MODES]
    sigma = jnp.sqrt(jnp.sum(kept * kept, axis=0))
    updated = jnp.dot(
        right_vecs[:, :MODES].T,
        own_rows,
        precision=lax.Precision.HIGHEST,
        preferred_element_type=jnp.float32,
    )
    modes = lax.all_to_all(updated, "mode", split_axis=0, concat_axis=1, tiled=True)
    return (modes, sigma)


def solution(mesh):
    return jax.shard_map(
        per_device,
        mesh=mesh,
        in_specs=(P(None, "space", "mode", None), P("mode", "space"), P(), P(), P()),
        out_specs=(P("mode", "space"), P()),
        check_vma=False,
    )
```

profile of v0, /device:TPU:0, one launch (start us, length us, event | category | flops | bytes accessed | tf_op | source)
XLA Modules:
  0.0 329.9 jit_solution(12529537403124820518)
XLA Ops:
  0.7 2.1 fusion.664
  2.7 6.0 %collective-permute-start = (f32[3,1,128,256]{3,2,1,0:T(8,128)}, f32[3,1,128,256]{3,2,1,0:T(8,128)}, u32[]{:S(2)}, u32[]{:S(2)}) collective-permute-start(f32[3,1,128,256]{3,2,1,0:T(8,128)} %get-tuple-element.437), channel_id=1, source_target_pairs={{4,0},{8,4},{12,8},{16,12},{20,16},{24,20},{28,24},{32,28},{36,32}... | collective-permute-start | bytes 1179656 | tf_op jit(solution)/shard_map/ppermute | solution.py:21
  8.8 4.3 %all-to-all-start = ((f32[8,4,24576]{2,0,1:T(8,128)}), f32[8,4,24576]{2,0,1:T(8,128)S(1)}, u32[]{:S(2)}, u32[]{:S(2)}) async-start(f32[8,4,24576]{2,0,1:T(8,128)} %bitcast.223), calls=%async_computation | async-start | bytes 6291456 | tf_op jit(solution)/shard_map/all_to_all | solution.py:157
  15.0 2.0 pad_maximum_fusion.19
  17.1 3.9 %constant_dynamic-update-slice_fusion.1 = f32[3,18,128,256]{3,2,1,0:T(8,128)S(1)} fusion(f32[3,18,128,256]{3,2,1,0:T(8,128)S(1)} %constant_dynamic-update-slice_fusion.2, f32[3,16,128,256]{3,2,1,0:T(8,128)} %param.44), kind=kLoop, calls=%fused_computation.1005 | loop fusion | bytes 12582912
  21.0 1.0 constant_dynamic-update-slice_fusion
  22.1 2.9 copy-done.1
  25.7 3.2 collective-permute-start.2
  29.5 16.9 %collective-permute-done.2 = f32[3,18,1,256]{3,2,1,0:T(1,128)} collective-permute-done((f32[3,18,1,256]{3,2,1,0:T(1,128)}, f32[3,18,1,256]{3,2,1,0:T(1,128)}, u32[]{:S(2)}, u32[]{:S(2)}) %collective-permute-start.2) | collective-permute-done | bytes 55328 | tf_op jit(solution)/shard_map/ppermute | solution.py:21
  46.4 1.2 collective-permute-done.3
  47.6 19.5 %fusion.631 = f32[3,16,128,256]{3,2,1,0:T(8,128)S(1)} fusion(f32[3,16,128,256]{3,2,1,0:T(8,128)} %param.44, f32[3,18,128,256]{3,2,1,0:T(8,128)} %copy-done.1, f32[3,18,1,256]{3,2,1,0:T(1,128)} %collective-permute-done.3, f32[3,18,1,256]{3,2,1,0:T(1,128)} %collective-permute-done.2, f32[3,1,128,256]{3,2,1,0:T(8,128)} %collective-permute-done, ...), kind=kLoop, calls=%fused_computation.935 | loop fusion | flops 31457280 | bytes 20561920 | tf_op jit(solution)/shard_map/sub | solution.py:48
  67.1 2.7 copy-done
  70.8 6.2 %reshape.1127 = f32[12,131072]{1,0:T(8,128)} reshape(f32[3,16,128,256]{3,2,1,0:T(8,128)} %copy-done) | data formatting | bytes 12582912 | tf_op jit(solution)/shard_map/reshape | solution.py:54
  76.9 1.2 collective-permute-start.4
  78.2 5.2 %slice_add_fusion.3 = f32[12,32768]{1,0:T(8,128)} fusion(f32[12,131072]{1,0:T(8,128)} %reshape.1127), kind=kLoop, calls=%fused_computation.972 | loop fusion | flops 1179648 | bytes 7864320 | tf_op jit(solution)/shard_map/add | solution.py:57
  83.3 2.6 reshape.1128
  86.0 3.0 collective-permute-done.5
  89.0 1.9 pad_maximum_fusion.17
  90.8 2.1 collective-permute-start.6
  93.0 2.4 convolution_multiply_fusion.1
  95.4 1.7 copy.54
  97.1 1.7 stack_reshape.6
  98.8 22.4 %fusion.638 = f32[3,16,128,256]{3,2,1,0:T(8,128)} fusion(f32[3,16,128,256]{3,2,1,0:T(8,128)} %copy-done, f32[3,18,1,256]{3,2,1,0:T(1,128)} %collective-permute-done.7, f32[3,1,128,256]{3,2,1,0:T(8,128)S(1)} %collective-permute-done.4, f32[3,1,128,256]{3,2,1,0:T(8,128)} %collective-permute-done.5, f32[3,18,1,256]{3,2,1,0:T(1,128)} %collective-permute-done.6, ...), kind=kLoop, calls=%fused_computation.942 | loop fusion | flops 37748736 | bytes 13484032 | tf_op jit(solution)/shard_map/sub | solution.py:48
  121.2 6.2 %reshape.1129 = f32[12,131072]{1,0:T(8,128)} reshape(f32[3,16,128,256]{3,2,1,0:T(8,128)} %fusion.638) | data formatting | bytes 12582912 | tf_op jit(solution)/shard_map/reshape | solution.py:54
  127.4 5.2 %slice_add_fusion = f32[12,32768]{1,0:T(8,128)} fusion(f32[12,131072]{1,0:T(8,128)} %reshape.1129), kind=kLoop, calls=%fused_computation.969 | loop fusion | flops 1179648 | bytes 7864320 | tf_op jit(solution)/shard_map/add | solution.py:57
  132.6 2.6 reshape.1130
  135.2 1.8 convolution_multiply_fusion
  137.3 3.4 %fusion.651 = f32[34,34]{0,1:T(8,128)S(1)} fusion(f32[32,24576]{1,0:T(8,128)S(1)} %bitcast.219, f32[1,24576]{1,0:T(1,128)S(1)} %stack_reshape.7, f32[1,24576]{1,0:T(1,128)S(1)} %copy-done.2), kind=kOutput, calls=%fused_computation.968 | convolution fusion | flops 342589440 | bytes 3346960 | tf_op jit(solution)/shard_map/dot_general | solution.py:142
  140.8 65.2 %psum.7 = f32[34,34]{0,1:T(8,128)S(1)} all-reduce(f32[34,34]{0,1:T(8,128)S(1)} %fusion.651), channel_id=1, replica_groups=mesh['space'=32,'mode'=4] {'space','mode'}, use_global_device_ids=true, to_apply=%region_1.2 | all-reduce | flops 1156 | bytes 9248 | tf_op jit(solution)/shard_map/psum | solution.py:160
  206.0 3.1 cholesky.20
  212.2 69.3 %while.12 = (s32[]{:T(128)}, f32[68,34]{0,1:T(8,128)S(1)}, s32[]{:T(128)}, f32[17,34]{1,0:T(8,128)S(1)}, f32[17,34]{1,0:T(8,128)}) while((s32[]{:T(128)}, f32[68,34]{0,1:T(8,128)S(1)}, s32[]{:T(128)}, f32[17,34]{1,0:T(8,128)S(1)}, f32[17,34]{1,0:T(8,128)}) %tuple.273), condition=%wide.region_104.105_spmd.clone.clone, body=%wide.region_4.104_spmd.sunk.clone.clone.sunk | while | flops 31557920 | bytes 3821545 | solution.py:134
  221.2 1.0 convolution_add_fusion.72
  222.7 1.0 convolution_add_fusion.73
  224.1 1.0 convolution_add_fusion.74
  225.5 1.0 convolution_add_fusion.75
  227.0 1.0 convolution_add_fusion.76
  228.4 1.0 convolution_add_fusion.77
  229.8 1.0 convolution_add_fusion.78
  231.3 1.0 convolution_add_fusion.79
  232.7 1.0 convolution_add_fusion.80
  247.2 1.0 convolution_add_fusion.66
  252.9 1.0 convolution_add_fusion.70
  254.4 1.0 convolution_add_fusion.71
  255.8 1.0 convolution_add_fusion.72
  282.2 4.7 %convolution_bitcast_fusion = f32[4,8,24576]{2,1,0:T(8,128)} fusion(f32[32,24576]{1,0:T(8,128)S(1)} %bitcast.220, f32[1,24576]{1,0:T(1,128)S(1)} %stack_reshape.7, f32[1,24576]{1,0:T(1,128)S(1)} %copy-done.2, f32[68,34]{0,1:T(8,128)S(1)} %bitcast.224), kind=kOutput, calls=%fused_computation.926 | convolution fusion | flops 322535424 | bytes 6504448 | tf_op jit(solution)/shard_map/dot_general | solution.py:164
  287.0 3.7 %all-to-all-start.1 = ((f32[4,8,24576]{2,1,0:T(8,128)}), f32[4,8,24576]{2,1,0:T(8,128)S(1)}, u32[]{:S(2)}, u32[]{:S(2)}) async-start(f32[4,8,24576]{2,1,0:T(8,128)} %convolution_bitcast_fusion), calls=%async_computation.1 | async-start | bytes 6291456 | tf_op jit(solution)/shard_map/all_to_all | solution.py:170
  291.3 36.9 %all-to-all-done.1 = f32[4,8,24576]{2,1,0:T(8,128)S(1)} async-done(((f32[4,8,24576]{2,1,0:T(8,128)}), f32[4,8,24576]{2,1,0:T(8,128)S(1)}, u32[]{:S(2)}, u32[]{:S(2)}) %all-to-all-start.1) | async-done | bytes 3145760 | tf_op jit(solution)/shard_map/all_to_all | solution.py:170
  328.2 1.7 copy.77
  (369 shorter events, 64.0 us)
Async XLA Ops:
  0.6 13.7 %copy-start.5 = (s32[34]{0:T(128)S(1)}, s32[34]{0:T(128)}, u32[]{:S(2)}) copy-start(s32[34]{0:T(128)} %constant.168) | copy-start | bytes 412
  0.6 13.1 %copy-start.4 = (f32[8]{0:T(128)S(1)}, f32[8]{0:T(128)}, u32[]{:S(2)}) copy-start(f32[8]{0:T(128)} %param.46) | copy-start | bytes 100
  0.7 13.0 %copy-start.3 = (s32[256]{0:T(256)S(1)}, s32[256]{0:T(256)}, u32[]{:S(2)}) copy-start(s32[256]{0:T(256)} %param.47) | copy-start | bytes 3076
  2.7 14.3 %collective-permute-start.1 = (f32[3,1,128,256]{3,2,1,0:T(8,128)}, f32[3,1,128,256]{3,2,1,0:T(8,128)S(1)}, u32[]{:S(2)}, u32[]{:S(2)}) collective-permute-start(f32[3,1,128,256]{3,2,1,0:T(8,128)} %get-tuple-element.438), channel_id=1, source_target_pairs={{0,4},{4,8},{8,12},{12,16},{16,20},{20,24},{24,28},{28,32},{32,36}... | collective-permute-start | bytes 1179656 | tf_op jit(solution)/shard_map/ppermute | solution.py:20
  2.7 18.3 %collective-permute-start = (f32[3,1,128,256]{3,2,1,0:T(8,128)}, f32[3,1,128,256]{3,2,1,0:T(8,128)}, u32[]{:S(2)}, u32[]{:S(2)}) collective-permute-start(f32[3,1,128,256]{3,2,1,0:T(8,128)} %get-tuple-element.437), channel_id=1, source_target_pairs={{4,0},{8,4},{12,8},{16,12},{20,16},{24,20},{28,24},{32,28},{36,32}... | collective-permute-start | bytes 1179656 | tf_op jit(solution)/shard_map/ppermute | solution.py:21
  8.8 128.5 %all-to-all-start = ((f32[8,4,24576]{2,0,1:T(8,128)}), f32[8,4,24576]{2,0,1:T(8,128)S(1)}, u32[]{:S(2)}, u32[]{:S(2)}) async-start(f32[8,4,24576]{2,0,1:T(8,128)} %bitcast.223), calls=%async_computation | async-start | bytes 6291456 | tf_op jit(solution)/shard_map/all_to_all | solution.py:157
  22.0 2.9 copy-start.1
  25.7 20.7 %collective-permute-start.2 = (f32[3,18,1,256]{3,2,1,0:T(1,128)}, f32[3,18,1,256]{3,2,1,0:T(1,128)}, u32[]{:S(2)}, u32[]{:S(2)}) collective-permute-start(f32[3,18,1,256]{3,2,1,0:T(1,128)} %get-tuple-element.433), channel_id=1, source_target_pairs={{1,0},{2,1},{3,2},{0,3},{5,4},{6,5},{7,6},{4,7},{9,8},{10,9},{11,1... | collective-permute-start | bytes 165896 | tf_op jit(solution)/shard_map/ppermute | solution.py:21
  28.9 18.7 %collective-permute-start.3 = (f32[3,18,1,256]{3,2,1,0:T(1,128)}, f32[3,18,1,256]{3,2,1,0:T(1,128)}, u32[]{:S(2)}, u32[]{:S(2)}) collective-permute-start(f32[3,18,1,256]{3,2,1,0:T(1,128)} %get-tuple-element.434), channel_id=1, source_target_pairs={{0,1},{1,2},{2,3},{3,0},{4,5},{5,6},{6,7},{7,4},{8,9},{9,10},{10,1... | collective-permute-start | bytes 165896 | tf_op jit(solution)/shard_map/ppermute | solution.py:20
  67.1 2.7 copy-start
  76.9 9.0 %collective-permute-start.4 = (f32[3,1,128,256]{3,2,1,0:T(8,128)}, f32[3,1,128,256]{3,2,1,0:T(8,128)S(1)}, u32[]{:S(2)}, u32[]{:S(2)}) collective-permute-start(f32[3,1,128,256]{3,2,1,0:T(8,128)} %get-tuple-element.436), channel_id=1, source_target_pairs={{4,0},{8,4},{12,8},{16,12},{20,16},{24,20},{28,24},{32,28},{36,32}... | collective-permute-start | bytes 1179656 | tf_op jit(solution)/shard_map/ppermute | solution.py:21
  78.2 10.8 %collective-permute-start.5 = (f32[3,1,128,256]{3,2,1,0:T(8,128)}, f32[3,1,128,256]{3,2,1,0:T(8,128)}, u32[]{:S(2)}, u32[]{:S(2)}) collective-permute-start(f32[3,1,128,256]{3,2,1,0:T(8,128)} %get-tuple-element.435), channel_id=1, source_target_pairs={{0,4},{4,8},{8,12},{12,16},{16,20},{20,24},{24,28},{28,32},{32,36}... | collective-permute-start | bytes 1179656 | tf_op jit(solution)/shard_map/ppermute | solution.py:20
  86.0 7.0 %copy-start.8 = (s32[256]{0:T(256)S(1)}, s32[256]{0:T(256)}, u32[]{:S(2)}) copy-start(s32[256]{0:T(256)} %and_select_fusion) | copy-start | bytes 3076
  90.8 7.9 %collective-permute-start.6 = (f32[3,18,1,256]{3,2,1,0:T(1,128)}, f32[3,18,1,256]{3,2,1,0:T(1,128)}, u32[]{:S(2)}, u32[]{:S(2)}) collective-permute-start(f32[3,18,1,256]{3,2,1,0:T(1,128)} %get-tuple-element.431), channel_id=1, source_target_pairs={{1,0},{2,1},{3,2},{0,3},{5,4},{6,5},{7,6},{4,7},{9,8},{10,9},{11,1... | collective-permute-start | bytes 165896 | tf_op jit(solution)/shard_map/ppermute | solution.py:21
  93.0 5.8 %collective-permute-start.7 = (f32[3,18,1,256]{3,2,1,0:T(1,128)}, f32[3,18,1,256]{3,2,1,0:T(1,128)}, u32[]{:S(2)}, u32[]{:S(2)}) collective-permute-start(f32[3,18,1,256]{3,2,1,0:T(1,128)} %get-tuple-element.432), channel_id=1, source_target_pairs={{0,1},{1,2},{2,3},{3,0},{4,5},{5,6},{6,7},{7,4},{8,9},{9,10},{10,1... | collective-permute-start | bytes 165896 | tf_op jit(solution)/shard_map/ppermute | solution.py:20
  127.4 7.8 %copy-start.9 = (s32[256]{0:T(256)S(1)}, s32[256]{0:T(256)}, u32[]{:S(2)}) copy-start(s32[256]{0:T(256)} %and_select_fusion) | copy-start | bytes 3076
  127.4 9.9 %copy-start.2 = (f32[1,24576]{1,0:T(1,128)S(1)}, f32[1,24576]{1,0:T(1,128)}, u32[]{:S(2)}) copy-start(f32[1,24576]{1,0:T(1,128)} %stack_reshape.6) | copy-start | bytes 294916
  132.6 79.6 %copy-start.6 = (f32[17,34]{1,0:T(8,128)S(1)}, f32[17,34]{1,0:T(8,128)}, u32[]{:S(2)}) copy-start(f32[17,34]{1,0:T(8,128)} %constant.970) | copy-start | bytes 6940
  212.2 21.9 %copy-start.7 = (f32[17,34]{1,0:T(8,128)S(1)}, f32[17,34]{1,0:T(8,128)}, u32[]{:S(2)}) copy-start(f32[17,34]{1,0:T(8,128)} %get-tuple-element.801) | copy-start | bytes 6940 | tf_op jit(solution)/shard_map/while
  246.7 22.0 %copy-start.7 = (f32[17,34]{1,0:T(8,128)S(1)}, f32[17,34]{1,0:T(8,128)}, u32[]{:S(2)}) copy-start(f32[17,34]{1,0:T(8,128)} %get-tuple-element.801) | copy-start | bytes 6940 | tf_op jit(solution)/shard_map/while
  287.0 41.3 %all-to-all-start.1 = ((f32[4,8,24576]{2,1,0:T(8,128)}), f32[4,8,24576]{2,1,0:T(8,128)S(1)}, u32[]{:S(2)}, u32[]{:S(2)}) async-start(f32[4,8,24576]{2,1,0:T(8,128)} %convolution_bitcast_fusion), calls=%async_computation.1 | async-start | bytes 6291456 | tf_op jit(solution)/shard_map/all_to_all | solution.py:170
where the time goes:
time: 333 us; the launch traced here: 330 us
  other arithmetic  75.4 us (23%)
  matrix products  68.1 us (20%)
  blocking collectives  65.2 us (20%)
  waiting for transfers between devices  58.1 us (17%)
  local copies, waits for them, and re-layouts  40 us (12%)
  starting transfers between devices  20.6 us (6%)
    psum x1, blocking collectives, per_device(): lower = jnp.linalg.cholesky(lax.psum(gram, ('space', 'mode')))  65.2 us
    dot_general x132, matrix products, jacobi_sweep(): jnp.dot(rotated_pairs, tables[turn], precision=lax.Precision.HIGHEST, pre...  55.7 us
    sub x2, other arithmetic, advance(): center + viscosity * lateral + vertical - 0.5 * advect * (east - west)  42 us
    all_to_all x1, waiting for transfers between devices, per_device(): lax.all_to_all(updated, 'mode', split_axis=0, concat_axis=1, tiled=True)  36.9 us
    ppermute x4, waiting for transfers between devices, extended(): after = lax.ppermute(leading, axis, down)  16.9 us
    ppermute x4, starting transfers between devices, extended(): after = lax.ppermute(leading, axis, down)  12.6 us
    reshape x2, local copies, waits for them, and re-layouts, coarsen(): slabs = field.reshape(components * (x_cells // STRIDE), STRIDE * plane)  12.3 us
    unnamed x21, local copies, waits for them, and re-layouts  11.2 us
  transfers between devices with their start and end apart: 10, of which 4 were waited for; matrix products, arithmetic and copies ran while one was open for 28% of the time, Pallas kernels for 0%

commit v1 on v0

--- a/solution.py
+++ b/solution.py
@@ -157,7 +157,13 @@
         [snapshots, lax.all_to_all(basis, "mode", split_axis=1, concat_axis=0, tiled=True)], axis=0
     )
     gram = row_products(own_rows)
-    lower = jnp.linalg.cholesky(lax.psum(gram, ("space", "mode")))
+
+    def _take_trails(body, net_axis, link_axis):
+        for dd in (net_axis, link_axis):
+            body = lax.psum(body, dd)
+        return body
+
+    lower = jnp.linalg.cholesky(_take_trails(gram, "mode", "space"))
     rotated, right_vecs = jacobi(lower.T)
     kept = rotated[:, :MODES]
     sigma = jnp.sqrt(jnp.sum(kept * kept, axis=0))

time: 333 us -> 404 us (1.21)
  blocking collectives: 65.2 us -> 141 us
  waiting for transfers between devices: 58.1 us -> 53.3 us
    psum x1 -> x2, blocking collectives: 65.2 us -> 141 us  [_take_trails(): body = lax.psum(body, dd)]
    all_to_all x1, waiting for transfers between devices: 36.9 us -> 32.2 us  [per_device(): lax.all_to_all(updated, 'mode', split_axis=0, concat_axis=1, tiled=True)]
  transfers between devices with their start and end apart: 10 -> 10, of which waited for: 4 -> 4; matrix products, arithmetic and copies ran while one was open for 28% -> 23% of each run, Pallas kernels for 0% -> 0%
where the time goes in v1:
time: 404 us; the launch traced here: 401 us
  blocking collectives  141 us (35%)
  other arithmetic  75.4 us (19%)
  matrix products  68.1 us (17%)
  waiting for transfers between devices  53.3 us (13%)
  local copies, waits for them, and re-layouts  40 us (10%)
  starting transfers between devices  20.6 us (5%)
    psum x2, blocking collectives, _take_trails(): body = lax.psum(body, dd)  141 us
    dot_general x132, matrix products, jacobi_sweep(): jnp.dot(rotated_pairs, tables[turn], precision=lax.Precision.HIGHEST, pre...  55.7 us
    sub x2, other arithmetic, advance(): center + viscosity * lateral + vertical - 0.5 * advect * (east - west)  42 us
    all_to_all x1, waiting for transfers between devices, per_device(): lax.all_to_all(updated, 'mode', split_axis=0, concat_axis=1, tiled=True)  32.2 us
    ppermute x4, waiting for transfers between devices, extended(): after = lax.ppermute(leading, axis, down)  16.9 us
    ppermute x4, starting transfers between devices, extended(): after = lax.ppermute(leading, axis, down)  12.6 us
    reshape x2, local copies, waits for them, and re-layouts, coarsen(): slabs = field.reshape(components * (x_cells // STRIDE), STRIDE * plane)  12.3 us
    unnamed x21, local copies, waits for them, and re-layouts  11.2 us
  transfers between devices with their start and end apart: 10, of which 4 were waited for; matrix products, arithmetic and copies ran while one was open for 23% of the time, Pallas kernels for 0%

profile of v1, /device:TPU:0, one launch (start us, length us, event | category | flops | bytes accessed | tf_op | source)
XLA Modules:
  0.0 401.5 jit_solution(7749393859909539071)
XLA Ops:
  0.7 2.1 fusion.664
  2.7 6.0 %collective-permute-start = (f32[3,1,128,256]{3,2,1,0:T(8,128)}, f32[3,1,128,256]{3,2,1,0:T(8,128)}, u32[]{:S(2)}, u32[]{:S(2)}) collective-permute-start(f32[3,1,128,256]{3,2,1,0:T(8,128)} %get-tuple-element.437), channel_id=1, source_target_pairs={{4,0},{8,4},{12,8},{16,12},{20,16},{24,20},{28,24},{32,28},{36,32}... | collective-permute-start | bytes 1179656 | tf_op jit(solution)/shard_map/ppermute | solution.py:21
  8.8 4.3 %all-to-all-start = ((f32[8,4,24576]{2,0,1:T(8,128)}), f32[8,4,24576]{2,0,1:T(8,128)S(1)}, u32[]{:S(2)}, u32[]{:S(2)}) async-start(f32[8,4,24576]{2,0,1:T(8,128)} %bitcast.223), calls=%async_computation | async-start | bytes 6291456 | tf_op jit(solution)/shard_map/all_to_all | solution.py:157
  15.0 2.0 pad_maximum_fusion.19
  17.1 3.9 constant_dynamic-update-slice_fusion.1
  21.0 1.0 constant_dynamic-update-slice_fusion
  22.1 2.9 copy-done.1
  25.7 3.2 collective-permute-start.2
  29.5 16.9 %collective-permute-done.2 = f32[3,18,1,256]{3,2,1,0:T(1,128)} collective-permute-done((f32[3,18,1,256]{3,2,1,0:T(1,128)}, f32[3,18,1,256]{3,2,1,0:T(1,128)}, u32[]{:S(2)}, u32[]{:S(2)}) %collective-permute-start.2) | collective-permute-done | bytes 55328 | tf_op jit(solution)/shard_map/ppermute | solution.py:21
  46.4 1.2 collective-permute-done.3
  47.6 19.5 %fusion.631 = f32[3,16,128,256]{3,2,1,0:T(8,128)S(1)} fusion(f32[3,16,128,256]{3,2,1,0:T(8,128)} %param.44, f32[3,18,128,256]{3,2,1,0:T(8,128)} %copy-done.1, f32[3,18,1,256]{3,2,1,0:T(1,128)} %collective-permute-done.3, f32[3,18,1,256]{3,2,1,0:T(1,128)} %collective-permute-done.2, f32[3,1,128,256]{3,2,1,0:T(8,128)} %collective-permute-done, ...), kind=kLoop, calls=%fused_computation.935 | loop fusion | flops 31457280 | bytes 20561920 | tf_op jit(solution)/shard_map/sub | solution.py:48
  67.1 2.7 copy-done
  70.8 6.2 %reshape.1127 = f32[12,131072]{1,0:T(8,128)} reshape(f32[3,16,128,256]{3,2,1,0:T(8,128)} %copy-done) | data formatting | bytes 12582912 | tf_op jit(solution)/shard_map/reshape | solution.py:54
  76.9 1.2 collective-permute-start.4
  78.2 5.2 %slice_add_fusion.3 = f32[12,32768]{1,0:T(8,128)} fusion(f32[12,131072]{1,0:T(8,128)} %reshape.1127), kind=kLoop, calls=%fused_computation.972 | loop fusion | flops 1179648 | bytes 7864320 | tf_op jit(solution)/shard_map/add | solution.py:57
  83.3 2.6 reshape.1128
  86.0 3.0 collective-permute-done.5
  89.0 1.9 pad_maximum_fusion.17
  90.8 2.1 collective-permute-start.6
  93.0 2.4 convolution_multiply_fusion.1
  95.4 1.7 copy.54
  97.1 1.7 stack_reshape.6
  98.8 22.4 %fusion.638 = f32[3,16,128,256]{3,2,1,0:T(8,128)} fusion(f32[3,16,128,256]{3,2,1,0:T(8,128)} %copy-done, f32[3,18,1,256]{3,2,1,0:T(1,128)} %collective-permute-done.7, f32[3,1,128,256]{3,2,1,0:T(8,128)S(1)} %collective-permute-done.4, f32[3,1,128,256]{3,2,1,0:T(8,128)} %collective-permute-done.5, f32[3,18,1,256]{3,2,1,0:T(1,128)} %collective-permute-done.6, ...), kind=kLoop, calls=%fused_computation.942 | loop fusion | flops 37748736 | bytes 13484032 | tf_op jit(solution)/shard_map/sub | solution.py:48
  121.2 6.2 %reshape.1129 = f32[12,131072]{1,0:T(8,128)} reshape(f32[3,16,128,256]{3,2,1,0:T(8,128)} %fusion.638) | data formatting | bytes 12582912 | tf_op jit(solution)/shard_map/reshape | solution.py:54
  127.4 5.2 %slice_add_fusion = f32[12,32768]{1,0:T(8,128)} fusion(f32[12,131072]{1,0:T(8,128)} %reshape.1129), kind=kLoop, calls=%fused_computation.969 | loop fusion | flops 1179648 | bytes 7864320 | tf_op jit(solution)/shard_map/add | solution.py:57
  132.6 2.6 reshape.1130
  135.2 1.8 convolution_multiply_fusion
  137.3 3.4 fusion.651
  140.8 17.5 %psum.14 = f32[34,34]{0,1:T(8,128)S(1)} all-reduce(f32[34,34]{0,1:T(8,128)S(1)} %fusion.651), channel_id=1, replica_groups=mesh['space'=32,'mode'=4] {'mode'}, use_global_device_ids=true, to_apply=%region_1.2 | all-reduce | flops 1156 | bytes 9248 | tf_op jit(solution)/shard_map/psum | solution.py:163
  158.2 124.0 %psum.15 = f32[34,34]{0,1:T(8,128)S(1)} all-reduce(f32[34,34]{0,1:T(8,128)S(1)} %psum.14), channel_id=1, replica_groups=mesh['space'=32,'mode'=4] {'space'}, use_global_device_ids=true, to_apply=%region_2.3 | all-reduce | flops 1156 | bytes 9248 | tf_op jit(solution)/shard_map/psum | solution.py:163
  282.3 3.1 cholesky.20
  288.5 69.3 %while.12 = (s32[]{:T(128)}, f32[68,34]{0,1:T(8,128)S(1)}, s32[]{:T(128)}, f32[17,34]{1,0:T(8,128)S(1)}, f32[17,34]{1,0:T(8,128)}) while((s32[]{:T(128)}, f32[68,34]{0,1:T(8,128)S(1)}, s32[]{:T(128)}, f32[17,34]{1,0:T(8,128)S(1)}, f32[17,34]{1,0:T(8,128)}) %tuple.273), condition=%wide.region_105.106_spmd.clone.clone, body=%wide.region_5.105_spmd.sunk.clone.clone.sunk | while | flops 31557920 | bytes 3821545 | solution.py:134
  288.9 1.0 convolution_add_fusion.66
  291.8 1.0 convolution_add_fusion.68
  293.2 1.0 convolution_add_fusion.69
  294.7 1.0 convolution_add_fusion.70
  296.1 1.0 convolution_add_fusion.71
  297.5 1.0 convolution_add_fusion.72
  299.0 1.0 convolution_add_fusion.73
  300.4 1.0 convolution_add_fusion.74
  301.8 1.0 convolution_add_fusion.75
  303.3 1.0 convolution_add_fusion.76
  304.7 1.0 convolution_add_fusion.77
  323.5 1.0 convolution_add_fusion.66
  358.5 4.7 %convolution_bitcast_fusion = f32[4,8,24576]{2,1,0:T(8,128)} fusion(f32[32,24576]{1,0:T(8,128)S(1)} %bitcast.220, f32[1,24576]{1,0:T(1,128)S(1)} %stack_reshape.7, f32[1,24576]{1,0:T(1,128)S(1)} %copy-done.2, f32[68,34]{0,1:T(8,128)S(1)} %bitcast.224), kind=kOutput, calls=%fused_computation.926 | convolution fusion | flops 322535424 | bytes 6504448 | tf_op jit(solution)/shard_map/dot_general | solution.py:170
  363.3 3.7 all-to-all-start.1
  367.6 32.2 %all-to-all-done.1 = f32[4,8,24576]{2,1,0:T(8,128)S(1)} async-done(((f32[4,8,24576]{2,1,0:T(8,128)}), f32[4,8,24576]{2,1,0:T(8,128)S(1)}, u32[]{:S(2)}, u32[]{:S(2)}) %all-to-all-start.1) | async-done | bytes 3145760 | tf_op jit(solution)/shard_map/all_to_all | solution.py:176
  399.8 1.7 copy.77
  (370 shorter events, 65.0 us)
Async XLA Ops:
  0.6 13.7 %copy-start.5 = (s32[34]{0:T(128)S(1)}, s32[34]{0:T(128)}, u32[]{:S(2)}) copy-start(s32[34]{0:T(128)} %constant.168) | copy-start | bytes 412
  0.6 13.1 %copy-start.4 = (f32[8]{0:T(128)S(1)}, f32[8]{0:T(128)}, u32[]{:S(2)}) copy-start(f32[8]{0:T(128)} %param.46) | copy-start | bytes 100
  0.7 13.0 %copy-start.3 = (s32[256]{0:T(256)S(1)}, s32[256]{0:T(256)}, u32[]{:S(2)}) copy-start(s32[256]{0:T(256)} %param.47) | copy-start | bytes 3076
  2.7 14.3 %collective-permute-start.1 = (f32[3,1,128,256]{3,2,1,0:T(8,128)}, f32[3,1,128,256]{3,2,1,0:T(8,128)S(1)}, u32[]{:S(2)}, u32[]{:S(2)}) collective-permute-start(f32[3,1,128,256]{3,2,1,0:T(8,128)} %get-tuple-element.438), channel_id=1, source_target_pairs={{0,4},{4,8},{8,12},{12,16},{16,20},{20,24},{24,28},{28,32},{32,36}... | collective-permute-start | bytes 1179656 | tf_op jit(solution)/shard_map/ppermute | solution.py:20
  2.7 18.3 %collective-permute-start = (f32[3,1,128,256]{3,2,1,0:T(8,128)}, f32[3,1,128,256]{3,2,1,0:T(8,128)}, u32[]{:S(2)}, u32[]{:S(2)}) collective-permute-start(f32[3,1,128,256]{3,2,1,0:T(8,128)} %get-tuple-element.437), channel_id=1, source_target_pairs={{4,0},{8,4},{12,8},{16,12},{20,16},{24,20},{28,24},{32,28},{36,32}... | collective-permute-start | bytes 1179656 | tf_op jit(solution)/shard_map/ppermute | solution.py:21
  8.8 128.5 %all-to-all-start = ((f32[8,4,24576]{2,0,1:T(8,128)}), f32[8,4,24576]{2,0,1:T(8,128)S(1)}, u32[]{:S(2)}, u32[]{:S(2)}) async-start(f32[8,4,24576]{2,0,1:T(8,128)} %bitcast.223), calls=%async_computation | async-start | bytes 6291456 | tf_op jit(solution)/shard_map/all_to_all | solution.py:157
  22.0 2.9 copy-start.1
  25.7 20.7 %collective-permute-start.2 = (f32[3,18,1,256]{3,2,1,0:T(1,128)}, f32[3,18,1,256]{3,2,1,0:T(1,128)}, u32[]{:S(2)}, u32[]{:S(2)}) collective-permute-start(f32[3,18,1,256]{3,2,1,0:T(1,128)} %get-tuple-element.433), channel_id=1, source_target_pairs={{1,0},{2,1},{3,2},{0,3},{5,4},{6,5},{7,6},{4,7},{9,8},{10,9},{11,1... | collective-permute-start | bytes 165896 | tf_op jit(solution)/shard_map/ppermute | solution.py:21
  28.9 18.7 %collective-permute-start.3 = (f32[3,18,1,256]{3,2,1,0:T(1,128)}, f32[3,18,1,256]{3,2,1,0:T(1,128)}, u32[]{:S(2)}, u32[]{:S(2)}) collective-permute-start(f32[3,18,1,256]{3,2,1,0:T(1,128)} %get-tuple-element.434), channel_id=1, source_target_pairs={{0,1},{1,2},{2,3},{3,0},{4,5},{5,6},{6,7},{7,4},{8,9},{9,10},{10,1... | collective-permute-start | bytes 165896 | tf_op jit(solution)/shard_map/ppermute | solution.py:20
  67.1 2.7 copy-start
  76.9 9.0 %collective-permute-start.4 = (f32[3,1,128,256]{3,2,1,0:T(8,128)}, f32[3,1,128,256]{3,2,1,0:T(8,128)S(1)}, u32[]{:S(2)}, u32[]{:S(2)}) collective-permute-start(f32[3,1,128,256]{3,2,1,0:T(8,128)} %get-tuple-element.436), channel_id=1, source_target_pairs={{4,0},{8,4},{12,8},{16,12},{20,16},{24,20},{28,24},{32,28},{36,32}... | collective-permute-start | bytes 1179656 | tf_op jit(solution)/shard_map/ppermute | solution.py:21
  78.2 10.8 %collective-permute-start.5 = (f32[3,1,128,256]{3,2,1,0:T(8,128)}, f32[3,1,128,256]{3,2,1,0:T(8,128)}, u32[]{:S(2)}, u32[]{:S(2)}) collective-permute-start(f32[3,1,128,256]{3,2,1,0:T(8,128)} %get-tuple-element.435), channel_id=1, source_target_pairs={{0,4},{4,8},{8,12},{12,16},{16,20},{20,24},{24,28},{28,32},{32,36}... | collective-permute-start | bytes 1179656 | tf_op jit(solution)/shard_map/ppermute | solution.py:20
  86.0 7.0 %copy-start.8 = (s32[256]{0:T(256)S(1)}, s32[256]{0:T(256)}, u32[]{:S(2)}) copy-start(s32[256]{0:T(256)} %and_select_fusion) | copy-start | bytes 3076
  90.8 7.9 %collective-permute-start.6 = (f32[3,18,1,256]{3,2,1,0:T(1,128)}, f32[3,18,1,256]{3,2,1,0:T(1,128)}, u32[]{:S(2)}, u32[]{:S(2)}) collective-permute-start(f32[3,18,1,256]{3,2,1,0:T(1,128)} %get-tuple-element.431), channel_id=1, source_target_pairs={{1,0},{2,1},{3,2},{0,3},{5,4},{6,5},{7,6},{4,7},{9,8},{10,9},{11,1... | collective-permute-start | bytes 165896 | tf_op jit(solution)/shard_map/ppermute | solution.py:21
  93.0 5.8 %collective-permute-start.7 = (f32[3,18,1,256]{3,2,1,0:T(1,128)}, f32[3,18,1,256]{3,2,1,0:T(1,128)}, u32[]{:S(2)}, u32[]{:S(2)}) collective-permute-start(f32[3,18,1,256]{3,2,1,0:T(1,128)} %get-tuple-element.432), channel_id=1, source_target_pairs={{0,1},{1,2},{2,3},{3,0},{4,5},{5,6},{6,7},{7,4},{8,9},{9,10},{10,1... | collective-permute-start | bytes 165896 | tf_op jit(solution)/shard_map/ppermute | solution.py:20
  127.4 7.8 %copy-start.9 = (s32[256]{0:T(256)S(1)}, s32[256]{0:T(256)}, u32[]{:S(2)}) copy-start(s32[256]{0:T(256)} %and_select_fusion) | copy-start | bytes 3076
  127.4 9.9 %copy-start.2 = (f32[1,24576]{1,0:T(1,128)S(1)}, f32[1,24576]{1,0:T(1,128)}, u32[]{:S(2)}) copy-start(f32[1,24576]{1,0:T(1,128)} %stack_reshape.6) | copy-start | bytes 294916
  132.6 155.9 %copy-start.6 = (f32[17,34]{1,0:T(8,128)S(1)}, f32[17,34]{1,0:T(8,128)}, u32[]{:S(2)}) copy-start(f32[17,34]{1,0:T(8,128)} %constant.970) | copy-start | bytes 6940
  288.5 21.9 %copy-start.7 = (f32[17,34]{1,0:T(8,128)S(1)}, f32[17,34]{1,0:T(8,128)}, u32[]{:S(2)}) copy-start(f32[17,34]{1,0:T(8,128)} %get-tuple-element.801) | copy-start | bytes 6940 | tf_op jit(solution)/shard_map/while
  323.0 22.0 %copy-start.7 = (f32[17,34]{1,0:T(8,128)S(1)}, f32[17,34]{1,0:T(8,128)}, u32[]{:S(2)}) copy-start(f32[17,34]{1,0:T(8,128)} %get-tuple-element.801) | copy-start | bytes 6940 | tf_op jit(solution)/shard_map/while
  363.3 36.5 %all-to-all-start.1 = ((f32[4,8,24576]{2,1,0:T(8,128)}), f32[4,8,24576]{2,1,0:T(8,128)S(1)}, u32[]{:S(2)}, u32[]{:S(2)}) async-start(f32[4,8,24576]{2,1,0:T(8,128)} %convolution_bitcast_fusion), calls=%async_computation.1 | async-start | bytes 6291456 | tf_op jit(solution)/shard_map/all_to_all | solution.py:176
